TPU v7x, 256 devices: a whole 4x4x8 slice. The times are simulated.
256 devices in a mesh: band: 4 (over y_lo, core), slab: 64 (over z, y_hi, x).
Axes of the slice: x: 4, y: 4 (y_hi: 2, y_lo: 2; y = y_hi * 2 + y_lo), z: 8, core: 2. Of those that a mesh axis runs over, the one named last changes fastest.
Arguments:
- bands: float32 [8, 192, 192, 192], P('band', 'slab'), may hold values from -8 to 8
- occupied: float32 [16, 192, 192, 192], P('band', 'slab'), may hold values from -8 to 8
- occ_index: int32 [2], replicated, may hold values from 0 to 15
- band_pick: int32 [8], P('band'), may hold values from 0 to 1
Outputs:
- exchange_out: float32 [8, 192, 192, 192], P('band', 'slab')
All inputs are finite; a program needn't handle non-finite values.
Results may differ from a plain program's by a relative error of at most 0.0001.
Values sent between devices are 32-bit elements; how exact they have to be, the bound alone decides.
A program may use at most 64 MiB of HBM per device.

v0:
```python
import math
import jax
import jax.numpy as jnp
from jax import lax
from jax.sharding import PartitionSpec as P

grid_step = 0.25
omega = 0.106


def broadcast(x, axis, root):
    mine = lax.axis_index(axis) == root
    return lax.psum(jnp.where(mine, x, jnp.zeros_like(x)), axis)


def wave_squared(length):
    modes = jnp.arange(length, dtype=jnp.int32)
    signed = jnp.where(modes <= length // 2, modes, modes - length)
    wave = 2.0 * math.pi / (length * grid_step) * signed.astype(jnp.float32)
    return wave * wave


def screened(squares):
    nonzero = jnp.where(squares > 0, squares, jnp.ones_like(squares))
    value = 4.0 * math.pi * (1.0 - jnp.exp(-squares / (4.0 * omega * omega))) / nonzero
    return jnp.where(squares > 0, value, jnp.full_like(squares, math.pi / (omega * omega)))


def cas_matrix(length):
    indices = jnp.arange(length, dtype=jnp.int32)
    product = indices[:, None] * indices[None, :] % length
    phases = 2.0 * math.pi / length * product.astype(jnp.float32)
    return jnp.cos(phases) + jnp.sin(phases)


def along_z(values, matrix):
    return jnp.einsum("pxyz,zk->pxyk", values, matrix, precision=lax.Precision.HIGHEST)


def along_y(values, matrix):
    return jnp.einsum("pxyz,yk->pxkz", values, matrix, precision=lax.Precision.HIGHEST)


def along_x(values, matrix):
    return jnp.einsum("pxyz,xk->pkyz", values, matrix, precision=lax.Precision.HIGHEST)


def shards(bands, occupied, occ_index, band_pick):
    points = bands.shape[2]
    planes = bands.shape[1]
    window = occ_index.shape[0]
    per_group = occupied.shape[0]
    matrix = cas_matrix(points)
    squares = wave_squared(points)
    offset = lax.axis_index("slab") * planes
    row_squares = lax.dynamic_slice_in_dim(squares, offset, planes)
    kernel = screened(squares[:, None, None] + row_squares[None, :, None] + squares[None, None, :])
    kernel = kernel / float(points * points * points)
    targets = jnp.take(bands, band_pick, axis=0)

    def fetch_orbital(turn):
        which = occ_index[turn]
        owner_group = which // per_group
        own_orbital = lax.dynamic_index_in_dim(occupied, which % per_group, 0, keepdims=False)
        return broadcast(own_orbital, "band", owner_group)

    def to_spectrum(density):
        return along_y(along_z(density, matrix), matrix)

    def from_spectrum(spectrum):
        return along_z(along_y(spectrum, matrix), matrix)

    def convolve(pencil):
        return along_x(kernel[None] * along_x(pencil, matrix), matrix)

    def back_each(pencil):
        return lax.all_to_all(convolve(pencil), "slab", split_axis=1, concat_axis=2, tiled=True)

    def update(turn, total):
        orbital = fetch_orbital(turn)
        density = targets * orbital[None]
        filtered = back_each(
            lax.all_to_all(to_spectrum(density), "slab", split_axis=2, concat_axis=1, tiled=True)
        )
        return total - from_spectrum(filtered) * orbital[None]

    result = lax.fori_loop(0, window, update, jnp.zeros(targets.shape, jnp.float32))
    return result


def solution(mesh):
    placed = (P("band", "slab", None, None), P("band", "slab", None, None), P(), P("band"))
    return jax.shard_map(
        shards, mesh=mesh, in_specs=placed, out_specs=P("band", "slab", None, None), check_vma=False
    )
```

profile of v0, /device:TPU:6, one launch (start us, length us, event | category | flops | bytes accessed | tf_op | source)
XLA Modules:
  0.0 321.0 jit_solution(7959825404634566891)
XLA Ops:
  6.5 0.1 dynamic_slice.24
  6.6 0.1 broadcast_add_fusion
  6.7 0.7 compare_select_fusion.1
  7.4 0.4 copy-done
  7.8 0.6 gather_fusion
  8.5 0.0 copy-done.6
  8.5 0.2 broadcast_select_fusion
  8.7 0.5 copy-done.7
  9.1 305.0 %while.17 = (s32[]{:T(128)}, f32[2,3,192,192]{3,2,1,0:T(8,128)}, s32[2]{0:T(128)S(1)}, f32[4,3,192,192]{3,2,1,0:T(8,128)}, f32[2,3,192,192]{3,2,1,0:T(8,128)S(1)...) while((s32[]{:T(128)}, f32[2,3,192,192]{3,2,1,0:T(8,128)}, ...), condition=%wide.region_2.3_spmd.clone.clone, body=%wide.region_0.2_spmd.clone.clone.sunk | while | flops 3062292480 | bytes 46599840 | solution.py:87
  9.1 0.6 dynamic_slice.33
  12.0 1.9 select_bitcast_fusion.2
  13.9 0.0 all-reduce.2.cloned.1.call-update
  14.0 46.4 %all-reduce.2.cloned.1.call-done = f32[3,192,192]{2,1,0:T(8,128)} async-done(((f32[3,192,192]{2,1,0:T(8,128)}), f32[3,192,192]{2,1,0:T(8,128)}) %all-reduce.2.cloned.1.call-update) | async-done | bytes 442384 | tf_op jit(solution)/shard_map/while/body/eval_jaxpr/psum | solution.py:13
  60.4 3.1 fusion.81
  63.5 1.9 convolution_bitcast_fusion.7
  65.4 1.6 copy.44
  67.0 12.7 %all-to-all-start = ((f32[2,3,192,192]{3,0,1,2:T(2,128)}), f32[2,3,192,192]{3,0,1,2:T(2,128)S(1)}, u32[]{:S(2)}, u32[]{:S(2)}) async-start(f32[2,3,192,192]{3,0,1,2:T(2,128)} %copy.44), calls=%async_computation | async-start | bytes 2359296 | tf_op jit(solution)/shard_map/while/body/eval_jaxpr/all_to_all | solution.py:83
  79.7 0.3 fusion.82
  80.0 32.1 %all-to-all-done = f32[2,3,192,192]{3,0,1,2:T(2,128)S(1)} async-done(((f32[2,3,192,192]{3,0,1,2:T(2,128)}), f32[2,3,192,192]{3,0,1,2:T(2,128)S(1)}, u32[]{:S(2)}, u32[]{:S(2)}) %all-to-all-start) | async-done | bytes 884768 | tf_op jit(solution)/shard_map/while/body/eval_jaxpr/all_to_all | solution.py:83
  112.1 0.4 copy.45
  112.5 3.0 fusion.83
  115.5 1.9 convolution_bitcast_fusion.8
  117.4 1.6 copy.46
  119.0 7.2 %all-to-all-start.1 = ((f32[2,192,3,192]{3,0,2,1:T(2,128)}), f32[2,192,3,192]{3,0,2,1:T(2,128)S(1)}, u32[]{:S(2)}, u32[]{:S(2)}) async-start(f32[2,192,3,192]{3,0,2,1:T(2,128)} %copy.46), calls=%async_computation.1 | async-start | bytes 2359296 | tf_op jit(solution)/shard_map/while/body/eval_jaxpr/all_to_all | solution.py:77
  126.3 31.1 %all-to-all-done.1 = f32[2,192,3,192]{3,0,2,1:T(2,128)S(1)} async-done(((f32[2,192,3,192]{3,0,2,1:T(2,128)}), f32[2,192,3,192]{3,0,2,1:T(2,128)S(1)}, u32[]{:S(2)}, u32[]{:S(2)}) %all-to-all-start.1) | async-done | bytes 884768 | tf_op jit(solution)/shard_map/while/body/eval_jaxpr/all_to_all | solution.py:77
  157.3 0.4 copy.47
  157.8 3.0 convolution_bitcast_fusion.9
  160.8 3.4 %fusion.84 = f32[2,3,192,192]{3,2,1,0:T(8,128)S(1)} fusion(f32[2,3,192,192]{2,3,1,0:T(8,128)S(1)} %convolution_bitcast_fusion.9, f32[2,3,192,192]{3,2,1,0:T(8,128)S(1)} %copy-done.4, f32[3,192,192]{2,1,0:T(8,128)S(1)} %copy-done.1, pred[]{:T(512)S(6)} %compare.14), kind=kOutput, calls=%fused_computation.4.clone.1 | convolution fusion | flops 510640128 | bytes 3096577 | tf_op jit(solution)/shard_map/while/body/eval_jaxpr/pxyz,zk->pxyk/dot_general | solution.py:37
  164.2 1.0 copy-done.5
  165.2 0.6 dynamic_slice.33
  168.1 1.9 select_bitcast_fusion.2
  170.1 39.2 %all-reduce.2.cloned.1.call-done = f32[3,192,192]{2,1,0:T(8,128)} async-done(((f32[3,192,192]{2,1,0:T(8,128)}), f32[3,192,192]{2,1,0:T(8,128)}) %all-reduce.2.cloned.1.call-update) | async-done | bytes 442384 | tf_op jit(solution)/shard_map/while/body/eval_jaxpr/psum | solution.py:13
  209.2 3.1 fusion.81
  212.4 1.9 convolution_bitcast_fusion.7
  214.3 1.6 copy.44
  215.9 12.7 %all-to-all-start = ((f32[2,3,192,192]{3,0,1,2:T(2,128)}), f32[2,3,192,192]{3,0,1,2:T(2,128)S(1)}, u32[]{:S(2)}, u32[]{:S(2)}) async-start(f32[2,3,192,192]{3,0,1,2:T(2,128)} %copy.44), calls=%async_computation | async-start | bytes 2359296 | tf_op jit(solution)/shard_map/while/body/eval_jaxpr/all_to_all | solution.py:83
  228.5 0.3 fusion.82
  228.9 32.1 %all-to-all-done = f32[2,3,192,192]{3,0,1,2:T(2,128)S(1)} async-done(((f32[2,3,192,192]{3,0,1,2:T(2,128)}), f32[2,3,192,192]{3,0,1,2:T(2,128)S(1)}, u32[]{:S(2)}, u32[]{:S(2)}) %all-to-all-start) | async-done | bytes 884768 | tf_op jit(solution)/shard_map/while/body/eval_jaxpr/all_to_all | solution.py:83
  260.9 0.4 copy.45
  261.3 3.0 fusion.83
  264.4 1.9 convolution_bitcast_fusion.8
  266.3 1.6 copy.46
  267.9 7.2 %all-to-all-start.1 = ((f32[2,192,3,192]{3,0,2,1:T(2,128)}), f32[2,192,3,192]{3,0,2,1:T(2,128)S(1)}, u32[]{:S(2)}, u32[]{:S(2)}) async-start(f32[2,192,3,192]{3,0,2,1:T(2,128)} %copy.46), calls=%async_computation.1 | async-start | bytes 2359296 | tf_op jit(solution)/shard_map/while/body/eval_jaxpr/all_to_all | solution.py:77
  275.1 31.1 %all-to-all-done.1 = f32[2,192,3,192]{3,0,2,1:T(2,128)S(1)} async-done(((f32[2,192,3,192]{3,0,2,1:T(2,128)}), f32[2,192,3,192]{3,0,2,1:T(2,128)S(1)}, u32[]{:S(2)}, u32[]{:S(2)}) %all-to-all-start.1) | async-done | bytes 884768 | tf_op jit(solution)/shard_map/while/body/eval_jaxpr/all_to_all | solution.py:77
  306.2 0.4 copy.47
  306.6 3.0 convolution_bitcast_fusion.9
  309.7 3.4 %fusion.84 = f32[2,3,192,192]{3,2,1,0:T(8,128)S(1)} fusion(f32[2,3,192,192]{2,3,1,0:T(8,128)S(1)} %convolution_bitcast_fusion.9, f32[2,3,192,192]{3,2,1,0:T(8,128)S(1)} %copy-done.4, f32[3,192,192]{2,1,0:T(8,128)S(1)} %copy-done.1, pred[]{:T(512)S(6)} %compare.14), kind=kOutput, calls=%fused_computation.4.clone.1 | convolution fusion | flops 510640128 | bytes 3096577 | tf_op jit(solution)/shard_map/while/body/eval_jaxpr/pxyz,zk->pxyk/dot_general | solution.py:37
  313.1 1.0 copy-done.5
  (28 shorter events, 0.1 us)
Async XLA Ops:
  6.5 1.3 copy-start
  7.8 0.7 copy-start.6
  8.5 0.7 copy-start.7
  9.1 51.2 %copy-start.2 = (f32[2,3,192,192]{3,2,1,0:T(8,128)}, f32[2,3,192,192]{3,2,1,0:T(8,128)S(1)}, u32[]{:S(2)}) copy-start(f32[2,3,192,192]{3,2,1,0:T(8,128)S(1)} %get-tuple-element.343) | copy-start | bytes 2654212 | tf_op jit(solution)/shard_map/while
  9.1 51.2 %all-reduce.2.cloned.1.call-start = ((), (), s32[]{:S(2)}) async-start(), calls=%async_computation.2 | async-start | bytes 1179648 | tf_op jit(solution)/shard_map/while/body/eval_jaxpr/psum | solution.py:13
  67.0 45.1 %all-to-all-start = ((f32[2,3,192,192]{3,0,1,2:T(2,128)}), f32[2,3,192,192]{3,0,1,2:T(2,128)S(1)}, u32[]{:S(2)}, u32[]{:S(2)}) async-start(f32[2,3,192,192]{3,0,1,2:T(2,128)} %copy.44), calls=%async_computation | async-start | bytes 2359296 | tf_op jit(solution)/shard_map/while/body/eval_jaxpr/all_to_all | solution.py:83
  119.0 38.3 %all-to-all-start.1 = ((f32[2,192,3,192]{3,0,2,1:T(2,128)}), f32[2,192,3,192]{3,0,2,1:T(2,128)S(1)}, u32[]{:S(2)}, u32[]{:S(2)}) async-start(f32[2,192,3,192]{3,0,2,1:T(2,128)} %copy.46), calls=%async_computation.1 | async-start | bytes 2359296 | tf_op jit(solution)/shard_map/while/body/eval_jaxpr/all_to_all | solution.py:77
  157.7 3.1 copy-start.1
  157.8 3.1 copy-start.4
  160.8 4.4 %copy-start.3 = (f32[2,3,192,192]{3,2,1,0:T(8,128)S(1)}, f32[2,3,192,192]{3,2,1,0:T(8,128)}, u32[]{:S(2)}) copy-start(f32[2,3,192,192]{3,2,1,0:T(8,128)} %copy-done.2) | copy-start | bytes 2654212 | tf_op jit(solution)/shard_map/while
  164.2 1.0 copy-start.5
  165.2 44.0 %copy-start.2 = (f32[2,3,192,192]{3,2,1,0:T(8,128)}, f32[2,3,192,192]{3,2,1,0:T(8,128)S(1)}, u32[]{:S(2)}) copy-start(f32[2,3,192,192]{3,2,1,0:T(8,128)S(1)} %get-tuple-element.343) | copy-start | bytes 2654212 | tf_op jit(solution)/shard_map/while
  165.2 44.0 %all-reduce.2.cloned.1.call-start = ((), (), s32[]{:S(2)}) async-start(), calls=%async_computation.2 | async-start | bytes 1179648 | tf_op jit(solution)/shard_map/while/body/eval_jaxpr/psum | solution.py:13
  215.9 45.1 %all-to-all-start = ((f32[2,3,192,192]{3,0,1,2:T(2,128)}), f32[2,3,192,192]{3,0,1,2:T(2,128)S(1)}, u32[]{:S(2)}, u32[]{:S(2)}) async-start(f32[2,3,192,192]{3,0,1,2:T(2,128)} %copy.44), calls=%async_computation | async-start | bytes 2359296 | tf_op jit(solution)/shard_map/while/body/eval_jaxpr/all_to_all | solution.py:83
  267.9 38.3 %all-to-all-start.1 = ((f32[2,192,3,192]{3,0,2,1:T(2,128)}), f32[2,192,3,192]{3,0,2,1:T(2,128)S(1)}, u32[]{:S(2)}, u32[]{:S(2)}) async-start(f32[2,192,3,192]{3,0,2,1:T(2,128)} %copy.46), calls=%async_computation.1 | async-start | bytes 2359296 | tf_op jit(solution)/shard_map/while/body/eval_jaxpr/all_to_all | solution.py:77
  306.6 3.1 copy-start.1
  306.6 3.1 copy-start.4
  309.7 4.4 %copy-start.3 = (f32[2,3,192,192]{3,2,1,0:T(8,128)S(1)}, f32[2,3,192,192]{3,2,1,0:T(8,128)}, u32[]{:S(2)}) copy-start(f32[2,3,192,192]{3,2,1,0:T(8,128)} %copy-done.2) | copy-start | bytes 2654212 | tf_op jit(solution)/shard_map/while
  313.1 1.0 copy-start.5
Sparse Core Ops, SparseCore 0:
  14.1 46.2 all-reduce.1
  170.2 38.9 all-reduce.1
where the time goes:
time: 322 us; the launch traced here: 321 us
  waiting for transfers between devices  212 us (66%)
  starting transfers between devices  39.9 us (12%)
  matrix products  32.8 us (10%)
  between operations  13.4 us (4%)
  local copies, waits for them, and re-layouts  12.8 us (4%)
  other arithmetic  5.52 us (2%)
  loops' own time  4.72 us (1%)
    psum x2, waiting for transfers between devices, broadcast(): return lax.psum(jnp.where(mine, x, jnp.zeros_like(x)), axis)  85.5 us
    all_to_all x2, waiting for transfers between devices, update(): lax.all_to_all(to_spectrum(density), 'slab', split_axis=2, concat_axis=1,...  64.2 us
    all_to_all x2, waiting for transfers between devices, back_each(): lax.all_to_all(convolve(pencil), 'slab', split_axis=1, concat_axis=2, til...  62.1 us
    all_to_all x2, starting transfers between devices, update(): lax.all_to_all(to_spectrum(density), 'slab', split_axis=2, concat_axis=1,...  25.4 us
    all_to_all x2, starting transfers between devices, back_each(): lax.all_to_all(convolve(pencil), 'slab', split_axis=1, concat_axis=2, til...  14.5 us
    dot_general x4, matrix products, along_z(): jnp.einsum('pxyz,zk->pxyk', values, matrix, precision=lax.Precision.HIGHEST)  13 us
    dot_general x4, matrix products, along_x(): jnp.einsum('pxyz,xk->pkyz', values, matrix, precision=lax.Precision.HIGHEST)  9.88 us
    dot_general x4, matrix products, along_y(): jnp.einsum('pxyz,yk->pxkz', values, matrix, precision=lax.Precision.HIGHEST)  9.88 us
  transfers between devices with their start and end apart: 6, of which 6 were waited for; matrix products, arithmetic and copies ran while one was open for 0% of the time, Pallas kernels for 0%

commit v1 on v0

--- a/solution.py
+++ b/solution.py
@@ -6,6 +6,12 @@
 
 grid_step = 0.25
 omega = 0.106
+
+
+def swap_blocks(x, mesh_axis, split, join):
+    pieces = jnp.split(x, lax.axis_size(mesh_axis), axis=split)
+    received = lax.all_to_all(jnp.stack(pieces), mesh_axis, 0, 0)
+    return jnp.concatenate(received, axis=join)
 
 
 def broadcast(x, axis, root):
@@ -79,9 +85,7 @@
     def update(turn, total):
         orbital = fetch_orbital(turn)
         density = targets * orbital[None]
-        filtered = back_each(
-            lax.all_to_all(to_spectrum(density), "slab", split_axis=2, concat_axis=1, tiled=True)
-        )
+        filtered = back_each(swap_blocks(to_spectrum(density), "slab", 2, 1))
         return total - from_spectrum(filtered) * orbital[None]
 
     result = lax.fori_loop(0, window, update, jnp.zeros(targets.shape, jnp.float32))

time: 322 us -> 323 us (level)
    another operation x0 -> x4, local copies, waits for them, and re-layouts: none -> 3.28 us  [swap_blocks(): received = lax.all_to_all(jnp.stack(pieces), mesh_axis, 0, 0)]
where the time goes in v1:
time: 323 us
  waiting for transfers between devices  212 us (66%)
  starting transfers between devices  39.8 us (12%)
  matrix products  32.7 us (10%)
  local copies, waits for them, and re-layouts  13.8 us (4%)
  between operations  13.4 us (4%)
  other arithmetic  5.52 us (2%)
  loops' own time  5.42 us (2%)
    psum x2, waiting for transfers between devices, broadcast(): return lax.psum(jnp.where(mine, x, jnp.zeros_like(x)), axis)  85.5 us
    all_to_all x2, waiting for transfers between devices, swap_blocks(): received = lax.all_to_all(jnp.stack(pieces), mesh_axis, 0, 0)  64.2 us
    all_to_all x2, waiting for transfers between devices, back_each(): lax.all_to_all(convolve(pencil), 'slab', split_axis=1, concat_axis=2, til...  62.1 us
    all_to_all x2, starting transfers between devices, swap_blocks(): received = lax.all_to_all(jnp.stack(pieces), mesh_axis, 0, 0)  25.4 us
    all_to_all x2, starting transfers between devices, back_each(): lax.all_to_all(convolve(pencil), 'slab', split_axis=1, concat_axis=2, til...  14.5 us
    dot_general x4, matrix products, along_z(): jnp.einsum('pxyz,zk->pxyk', values, matrix, precision=lax.Precision.HIGHEST)  12.7 us
    dot_general x4, matrix products, along_y(): jnp.einsum('pxyz,yk->pxkz', values, matrix, precision=lax.Precision.HIGHEST)  10.1 us
    dot_general x4, matrix products, along_x(): jnp.einsum('pxyz,xk->pkyz', values, matrix, precision=lax.Precision.HIGHEST)  9.89 us
  transfers between devices with their start and end apart: 6, of which 6 were waited for; matrix products, arithmetic and copies ran while one was open for 0% of the time, Pallas kernels for 0%

profile of v1, /device:TPU:6, one launch (start us, length us, event | category | flops | bytes accessed | tf_op | source)
XLA Modules:
  0.0 322.5 jit_solution(1843550927380560079)
XLA Ops:
  6.5 0.1 dynamic_slice.24
  6.6 0.1 broadcast_add_fusion
  6.7 0.7 compare_select_fusion.1
  7.4 0.4 copy-done
  7.8 0.6 gather_fusion
  8.5 0.0 copy-start.7
  8.5 0.2 broadcast_select_fusion
  8.7 0.4 copy-done.7
  9.1 306.6 %while.17 = (s32[]{:T(128)}, f32[2,3,192,192]{3,2,1,0:T(8,128)}, s32[2]{0:T(128)S(1)}, f32[4,3,192,192]{3,2,1,0:T(8,128)}, f32[2,3,192,192]{3,2,1,0:T(8,128)S(1)...) while((s32[]{:T(128)}, f32[2,3,192,192]{3,2,1,0:T(8,128)}, ...), condition=%wide.region_2.3_spmd.clone.clone, body=%wide.region_0.2_spmd.clone.clone.sunk | while | flops 3062292480 | bytes 47965344 | solution.py:91
  9.1 0.6 dynamic_slice.33
  12.0 1.9 select_bitcast_fusion.2
  13.9 0.0 all-reduce.2.cloned.1.call-update
  13.9 46.4 %all-reduce.2.cloned.1.call-done = f32[3,192,192]{2,1,0:T(8,128)} async-done(((f32[3,192,192]{2,1,0:T(8,128)}), f32[3,192,192]{2,1,0:T(8,128)}) %all-reduce.2.cloned.1.call-update) | async-done | bytes 442384 | tf_op jit(solution)/shard_map/while/body/eval_jaxpr/psum | solution.py:19
  60.3 3.0 fusion.81
  63.3 2.0 convolution_bitcast_fusion.7
  66.6 1.6 copy.40
  68.2 12.7 %all-to-all-start = ((f32[64,2,3,3,192]{4,1,3,2,0:T(2,128)}), f32[64,2,3,3,192]{4,1,3,2,0:T(2,128)S(1)}, u32[]{:S(2)}, u32[]{:S(2)}) async-start(f32[64,2,3,3,192]{4,1,3,2,0:T(2,128)} %copy.40), calls=%async_computation | async-start | bytes 2359296 | tf_op jit(solution)/shard_map/while/body/eval_jaxpr/all_to_all | solution.py:13
  80.9 0.3 fusion.82
  81.2 32.1 %all-to-all-done = f32[64,2,3,3,192]{4,1,3,2,0:T(2,128)S(1)} async-done(((f32[64,2,3,3,192]{4,1,3,2,0:T(2,128)}), f32[64,2,3,3,192]{4,1,3,2,0:T(2,128)S(1)}, u32[]{:S(2)}, u32[]{:S(2)}) %all-to-all-start) | async-done | bytes 884768 | tf_op jit(solution)/shard_map/while/body/eval_jaxpr/all_to_all | solution.py:13
  113.3 3.0 fusion.83
  116.3 1.9 convolution_bitcast_fusion.8
  118.2 1.6 copy.41
  119.8 7.2 %all-to-all-start.1 = ((f32[2,192,3,192]{3,0,2,1:T(2,128)}), f32[2,192,3,192]{3,0,2,1:T(2,128)S(1)}, u32[]{:S(2)}, u32[]{:S(2)}) async-start(f32[2,192,3,192]{3,0,2,1:T(2,128)} %copy.41), calls=%async_computation.1 | async-start | bytes 2359296 | tf_op jit(solution)/shard_map/while/body/eval_jaxpr/all_to_all | solution.py:83
  127.1 31.1 %all-to-all-done.1 = f32[2,192,3,192]{3,0,2,1:T(2,128)S(1)} async-done(((f32[2,192,3,192]{3,0,2,1:T(2,128)}), f32[2,192,3,192]{3,0,2,1:T(2,128)S(1)}, u32[]{:S(2)}, u32[]{:S(2)}) %all-to-all-start.1) | async-done | bytes 884768 | tf_op jit(solution)/shard_map/while/body/eval_jaxpr/all_to_all | solution.py:83
  158.1 0.4 copy.42
  158.5 0.0 copy-start.4
  158.6 3.0 convolution_bitcast_fusion.9
  161.6 3.4 %fusion.84 = f32[2,3,192,192]{3,2,1,0:T(8,128)S(1)} fusion(f32[2,3,192,192]{2,3,1,0:T(8,128)S(1)} %convolution_bitcast_fusion.9, f32[2,3,192,192]{3,2,1,0:T(8,128)S(1)} %copy-done.4, f32[3,192,192]{2,1,0:T(8,128)S(1)} %copy-done.1, pred[]{:T(512)S(6)} %compare.14), kind=kOutput, calls=%fused_computation.4.clone.1 | convolution fusion | flops 510640128 | bytes 3096577 | tf_op jit(solution)/shard_map/while/body/eval_jaxpr/pxyz,zk->pxyk/dot_general | solution.py:43
  165.0 1.0 copy-done.5
  166.0 0.6 dynamic_slice.33
  168.9 1.9 select_bitcast_fusion.2
  170.8 0.0 all-reduce.2.cloned.1.call-update
  170.9 39.1 %all-reduce.2.cloned.1.call-done = f32[3,192,192]{2,1,0:T(8,128)} async-done(((f32[3,192,192]{2,1,0:T(8,128)}), f32[3,192,192]{2,1,0:T(8,128)}) %all-reduce.2.cloned.1.call-update) | async-done | bytes 442384 | tf_op jit(solution)/shard_map/while/body/eval_jaxpr/psum | solution.py:19
  210.0 3.0 fusion.81
  213.0 2.0 convolution_bitcast_fusion.7
  216.2 1.6 copy.40
  217.8 12.7 %all-to-all-start = ((f32[64,2,3,3,192]{4,1,3,2,0:T(2,128)}), f32[64,2,3,3,192]{4,1,3,2,0:T(2,128)S(1)}, u32[]{:S(2)}, u32[]{:S(2)}) async-start(f32[64,2,3,3,192]{4,1,3,2,0:T(2,128)} %copy.40), calls=%async_computation | async-start | bytes 2359296 | tf_op jit(solution)/shard_map/while/body/eval_jaxpr/all_to_all | solution.py:13
  230.5 0.3 fusion.82
  230.8 32.1 %all-to-all-done = f32[64,2,3,3,192]{4,1,3,2,0:T(2,128)S(1)} async-done(((f32[64,2,3,3,192]{4,1,3,2,0:T(2,128)}), f32[64,2,3,3,192]{4,1,3,2,0:T(2,128)S(1)}, u32[]{:S(2)}, u32[]{:S(2)}) %all-to-all-start) | async-done | bytes 884768 | tf_op jit(solution)/shard_map/while/body/eval_jaxpr/all_to_all | solution.py:13
  262.9 3.0 fusion.83
  266.0 1.9 convolution_bitcast_fusion.8
  267.9 1.6 copy.41
  269.5 7.2 %all-to-all-start.1 = ((f32[2,192,3,192]{3,0,2,1:T(2,128)}), f32[2,192,3,192]{3,0,2,1:T(2,128)S(1)}, u32[]{:S(2)}, u32[]{:S(2)}) async-start(f32[2,192,3,192]{3,0,2,1:T(2,128)} %copy.41), calls=%async_computation.1 | async-start | bytes 2359296 | tf_op jit(solution)/shard_map/while/body/eval_jaxpr/all_to_all | solution.py:83
  276.7 31.1 %all-to-all-done.1 = f32[2,192,3,192]{3,0,2,1:T(2,128)S(1)} async-done(((f32[2,192,3,192]{3,0,2,1:T(2,128)}), f32[2,192,3,192]{3,0,2,1:T(2,128)S(1)}, u32[]{:S(2)}, u32[]{:S(2)}) %all-to-all-start.1) | async-done | bytes 884768 | tf_op jit(solution)/shard_map/while/body/eval_jaxpr/all_to_all | solution.py:83
  307.8 0.4 copy.42
  308.2 3.0 convolution_bitcast_fusion.9
  311.3 3.4 %fusion.84 = f32[2,3,192,192]{3,2,1,0:T(8,128)S(1)} fusion(f32[2,3,192,192]{2,3,1,0:T(8,128)S(1)} %convolution_bitcast_fusion.9, f32[2,3,192,192]{3,2,1,0:T(8,128)S(1)} %copy-done.4, f32[3,192,192]{2,1,0:T(8,128)S(1)} %copy-done.1, pred[]{:T(512)S(6)} %compare.14), kind=kOutput, calls=%fused_computation.4.clone.1 | convolution fusion | flops 510640128 | bytes 3096577 | tf_op jit(solution)/shard_map/while/body/eval_jaxpr/pxyz,zk->pxyk/dot_general | solution.py:43
  314.7 1.0 copy-done.5
  (154 shorter events, 1.9 us)
Async XLA Ops:
  6.5 1.3 copy-start
  6.5 1.9 copy-start.6
  8.5 0.7 copy-start.7
  9.1 54.2 %copy-start.2 = (f32[2,3,192,192]{3,2,1,0:T(8,128)}, f32[2,3,192,192]{3,2,1,0:T(8,128)S(1)}, u32[]{:S(2)}) copy-start(f32[2,3,192,192]{3,2,1,0:T(8,128)S(1)} %get-tuple-element.343) | copy-start | bytes 2654212 | tf_op jit(solution)/shard_map/while
  9.1 51.2 %all-reduce.2.cloned.1.call-start = ((), (), s32[]{:S(2)}) async-start(), calls=%async_computation.2 | async-start | bytes 1179648 | tf_op jit(solution)/shard_map/while/body/eval_jaxpr/psum | solution.py:19
  68.2 45.1 %all-to-all-start = ((f32[64,2,3,3,192]{4,1,3,2,0:T(2,128)}), f32[64,2,3,3,192]{4,1,3,2,0:T(2,128)S(1)}, u32[]{:S(2)}, u32[]{:S(2)}) async-start(f32[64,2,3,3,192]{4,1,3,2,0:T(2,128)} %copy.40), calls=%async_computation | async-start | bytes 2359296 | tf_op jit(solution)/shard_map/while/body/eval_jaxpr/all_to_all | solution.py:13
  119.8 38.3 %all-to-all-start.1 = ((f32[2,192,3,192]{3,0,2,1:T(2,128)}), f32[2,192,3,192]{3,0,2,1:T(2,128)S(1)}, u32[]{:S(2)}, u32[]{:S(2)}) async-start(f32[2,192,3,192]{3,0,2,1:T(2,128)} %copy.41), calls=%async_computation.1 | async-start | bytes 2359296 | tf_op jit(solution)/shard_map/while/body/eval_jaxpr/all_to_all | solution.py:83
  158.5 3.1 copy-start.1
  158.5 3.1 copy-start.4
  161.6 4.4 %copy-start.3 = (f32[2,3,192,192]{3,2,1,0:T(8,128)S(1)}, f32[2,3,192,192]{3,2,1,0:T(8,128)}, u32[]{:S(2)}) copy-start(f32[2,3,192,192]{3,2,1,0:T(8,128)} %copy-done.2) | copy-start | bytes 2654212 | tf_op jit(solution)/shard_map/while
  165.0 1.0 copy-start.5
  166.0 46.9 %copy-start.2 = (f32[2,3,192,192]{3,2,1,0:T(8,128)}, f32[2,3,192,192]{3,2,1,0:T(8,128)S(1)}, u32[]{:S(2)}) copy-start(f32[2,3,192,192]{3,2,1,0:T(8,128)S(1)} %get-tuple-element.343) | copy-start | bytes 2654212 | tf_op jit(solution)/shard_map/while
  166.0 44.0 %all-reduce.2.cloned.1.call-start = ((), (), s32[]{:S(2)}) async-start(), calls=%async_computation.2 | async-start | bytes 1179648 | tf_op jit(solution)/shard_map/while/body/eval_jaxpr/psum | solution.py:19
  217.8 45.1 %all-to-all-start = ((f32[64,2,3,3,192]{4,1,3,2,0:T(2,128)}), f32[64,2,3,3,192]{4,1,3,2,0:T(2,128)S(1)}, u32[]{:S(2)}, u32[]{:S(2)}) async-start(f32[64,2,3,3,192]{4,1,3,2,0:T(2,128)} %copy.40), calls=%async_computation | async-start | bytes 2359296 | tf_op jit(solution)/shard_map/while/body/eval_jaxpr/all_to_all | solution.py:13
  269.5 38.3 %all-to-all-start.1 = ((f32[2,192,3,192]{3,0,2,1:T(2,128)}), f32[2,192,3,192]{3,0,2,1:T(2,128)S(1)}, u32[]{:S(2)}, u32[]{:S(2)}) async-start(f32[2,192,3,192]{3,0,2,1:T(2,128)} %copy.41), calls=%async_computation.1 | async-start | bytes 2359296 | tf_op jit(solution)/shard_map/while/body/eval_jaxpr/all_to_all | solution.py:83
  308.2 3.1 copy-start.1
  308.2 3.1 copy-start.4
  311.3 4.4 %copy-start.3 = (f32[2,3,192,192]{3,2,1,0:T(8,128)S(1)}, f32[2,3,192,192]{3,2,1,0:T(8,128)}, u32[]{:S(2)}) copy-start(f32[2,3,192,192]{3,2,1,0:T(8,128)} %copy-done.2) | copy-start | bytes 2654212 | tf_op jit(solution)/shard_map/while
  314.7 1.0 copy-start.5
Sparse Core Ops, SparseCore 0:
  14.1 46.2 all-reduce.1
  171.0 38.9 all-reduce.1
